TPU v7x, 128 devices: a whole 4x4x4 slice. The times are simulated.
128 devices in a mesh: dp: 4 (over x), seq: 32 (over z, y, core).
Axes of the slice: x: 4, y: 4, z: 4, core: 2. Of those that a mesh axis runs over, the one named last changes fastest.
Arguments:
- conv_input: bfloat16 [16384, 5376], P(('dp', 'seq')), may hold values from -6 to 6
- doc_start: int32 [16384], P(('dp', 'seq')), may hold values 0 or 1
- conv_weight: float32 [4, 5376], replicated, may hold values from -3 to 3
- conv_bias: float32 [5376], replicated, may hold values from -0.5 to 0.5
- dt_raw: float32 [16384, 80], P(('dp', 'seq')), may hold values from -3 to 3
- dt_bias: float32 [80], replicated, may hold values from -5.5 to -4.2
- a_log: float32 [80], replicated, may hold values from -9 to 2, as said below
- skip_gain: float32 [80], replicated, may hold values from 0.5 to 1.5
- cotangent: bfloat16 [16384, 5120], P(('dp', 'seq')), may hold values from -6 to 6
Outputs:
- ssm_output: bfloat16 [16384, 5120], P(('dp', 'seq'))
- grad_input: bfloat16 [16384, 5376], P(('dp', 'seq'))
- grad_conv_weight: float32 [4, 5376], replicated
- grad_conv_bias: float32 [5376], replicated
- grad_dt_bias: float32 [80], replicated
- grad_a_log: float32 [80], replicated
- grad_skip_gain: float32 [80], replicated
Inputs may be any that keep to these rules, and one draw needn't show every extreme that they name: `doc_start`: 1 marks the first token of a document; documents may cross shard boundaries. One value per head; exp(a_log) lies between 25 / 4096 and 4.2, so that the per-token decay rates exp(a_log) * steps_dt run from under 1 / 4096 to about 1.1.
All inputs are finite; a program needn't handle non-finite values.
Results may differ from a plain program's by a relative error of at most 0.00115.
Values may be sent and summed in bfloat16 or wider, within the bound.
A program may use at most 320 MiB of HBM per device.

v0:
```python
import jax
import jax.numpy as jnp
from jax import lax
from jax.sharding import PartitionSpec as P

HEADS = 80
HEAD_DIM = 64
STATE = 128
CONV = 4
BLOCK = 64
INNER = 5120
exact_mode = lax.Precision.HIGHEST


def from_behind(array, axis, by):
    size = lax.axis_size(axis)
    pairs = [(i, i + by) for i in range(size) if 0 <= i + by < size]
    return lax.ppermute(array, axis, pairs)


def prefix(array, axis, combine, identity, reverse):
    size, place = (lax.axis_size(axis), lax.axis_index(axis))
    everything = jax.tree.map(lambda part: lax.all_gather(part, axis), array)
    start = jax.tree.map(
        lambda part, zero: jnp.broadcast_to(jnp.asarray(zero, part.dtype), part.shape),
        array,
        identity,
    )

    def step(k, before):
        at = size - 1 - k if reverse else k
        reached = at > place if reverse else at < place
        new = combine(before, jax.tree.map(lambda part: part[at], everything))
        return jax.tree.map(lambda a, b: jnp.where(reached, a, b), new, before)

    return lax.fori_loop(0, size, step, start)


def prepare_inputs(
    tail_rows, conv_input, doc_start, conv_weight, conv_bias, dt_raw, dt_bias, a_log
):
    row_count = conv_input.shape[0]
    extended = jnp.concatenate([tail_rows, conv_input], axis=0)
    resets = doc_start.astype(jnp.float32)
    segment = jnp.cumsum(resets)
    padded = jnp.concatenate([jnp.zeros((CONV - 1,), jnp.float32), segment])
    convolved = conv_bias[None, :] + conv_weight[CONV - 1][None, :] * extended[CONV - 1 :]
    for offset in range(1, CONV):
        first_row = CONV - 1 - offset
        tap_valid = (padded[first_row : first_row + row_count] == segment).astype(jnp.float32)
        convolved = (
            convolved
            + conv_weight[first_row][None, :]
            * extended[first_row : first_row + row_count]
            * tap_valid[:, None]
        )
    activated = jax.nn.silu(convolved)
    values_x = activated[:, :INNER].reshape(row_count, HEADS, HEAD_DIM)
    keys_b = activated[:, INNER : INNER + STATE]
    reads_c = activated[:, INNER + STATE :]
    steps_dt = jax.nn.softplus(dt_raw + dt_bias[None, :])
    log_decay = -jnp.exp(a_log)[None, :] * steps_dt
    return (values_x, keys_b, reads_c, steps_dt, log_decay)


def scan_block(carry, block_data):
    carry_state, skip_gain = carry
    values_x, keys_b, reads_c, steps_dt, log_decay, resets = block_data
    length = values_x.shape[0]
    segment = jnp.cumsum(resets)
    running = jnp.cumsum(log_decay, axis=0)
    positions = jnp.arange(length)
    causal = (positions[:, None] >= positions[None, :]) & (segment[:, None] == segment[None, :])
    spread_log = running.T[:, :, None] - running.T[:, None, :]
    within = jnp.where(causal[None], jnp.exp(jnp.where(causal[None], spread_log, 0.0)), 0.0)
    scores = jnp.dot(reads_c, keys_b.T, precision=exact_mode)
    weights = within * scores[None] * steps_dt.T[:, None, :]
    output = jnp.einsum("hts,shp->thp", weights, values_x, precision=exact_mode)
    untouched = (segment == 0).astype(running.dtype)
    entry_weight = jnp.exp(running) * untouched[:, None]
    output = (
        output
        + jnp.einsum("tn,hpn->thp", reads_c, carry_state, precision=exact_mode)
        * entry_weight[:, :, None]
    )
    output = output + skip_gain[None, :, None] * values_x
    last_segment = (segment == segment[length - 1]).astype(running.dtype)
    leave_weight = (
        jnp.exp(running[length - 1][None, :] - running) * last_segment[:, None] * steps_dt
    )
    through = jnp.exp(running[length - 1]) * untouched[length - 1]
    added = jnp.einsum(
        "shp,sn->hpn", leave_weight[:, :, None] * values_x, keys_b, precision=exact_mode
    )
    carry_state = carry_state * through[:, None, None] + added
    return ((carry_state, skip_gain), output)


def chain_blocks(values_x, keys_b, reads_c, steps_dt, log_decay, resets, skip_gain, start_state):
    row_count = values_x.shape[0]
    block_count = row_count // BLOCK
    pieces = tuple(
        (
            member.reshape((block_count, BLOCK) + member.shape[1:])
            for member in (values_x, keys_b, reads_c, steps_dt, log_decay, resets)
        )
    )
    stepper = jax.checkpoint(scan_block)
    (final_state, _), outputs = lax.scan(stepper, (start_state, skip_gain), pieces)
    return (outputs.reshape(row_count, INNER), final_state)


def join_states(earlier, later):
    return (earlier[0] * later[0], later[0][:, None, None] * earlier[1] + later[1])


def on_device(
    conv_input, doc_start, conv_weight, conv_bias, dt_raw, dt_bias, a_log, skip_gain, cotangent
):
    row_count = conv_input.shape[0]
    resets = doc_start.astype(jnp.float32)
    after = jnp.concatenate([1.0 - resets[row_count - CONV + 2 :], jnp.ones((1,), jnp.float32)])
    keep_rows = jnp.flip(jnp.cumprod(jnp.flip(after)))
    tail_out = conv_input[row_count - CONV + 1 :] * keep_rows[:, None].astype(jnp.bfloat16)
    tail_in = from_behind(tail_out, "seq", 1)

    def prepare_local(tail_rows, rows_value, weight_value, bias_value, dtb_value, alog_value):
        return prepare_inputs(
            tail_rows,
            rows_value,
            doc_start,
            weight_value,
            bias_value,
            dt_raw,
            dtb_value,
            alog_value,
        )

    prepared, pull_prep = jax.vjp(
        prepare_local,
        tail_in.astype(jnp.float32),
        conv_input.astype(jnp.float32),
        conv_weight,
        conv_bias,
        dt_bias,
        a_log,
    )
    values_x, keys_b, reads_c, steps_dt, log_decay = prepared
    zero_state = jnp.zeros((HEADS, HEAD_DIM, STATE), jnp.float32)

    def local_chain(x_value, b_value, c_value, dt_value, decay_value, gain_value):
        return chain_blocks(
            x_value, b_value, c_value, dt_value, decay_value, resets, gain_value, zero_state
        )

    (local_out, local_state), pull_chain = jax.vjp(
        local_chain, values_x, keys_b, reads_c, steps_dt, log_decay, skip_gain
    )

    def entering(decay_value):
        running = jnp.cumsum(decay_value, axis=0)
        untouched = (jnp.cumsum(resets) == 0).astype(running.dtype)
        return (
            jnp.exp(running) * untouched[:, None],
            jnp.exp(running[row_count - 1]) * untouched[row_count - 1],
        )

    entry_weight, through = entering(log_decay)
    upstream = cotangent.astype(jnp.float32)
    upstream_heads = upstream.reshape(row_count, HEADS, HEAD_DIM)
    adjoint_local = jnp.einsum(
        "thp,tn->hpn", upstream_heads * entry_weight[:, :, None], reads_c, precision=exact_mode
    )
    identity = (jnp.ones((HEADS,), jnp.float32), jnp.zeros((HEADS, HEAD_DIM, STATE), jnp.float32))
    incoming = prefix((through, local_state), "seq", join_states, identity, False)[1]
    adjoint_end = prefix((through, adjoint_local), "seq", join_states, identity, True)[1]

    def carried(c_value, decay_value):
        weight_in, through_in = entering(decay_value)
        added = (
            jnp.einsum("tn,hpn->thp", c_value, incoming, precision=exact_mode)
            * weight_in[:, :, None]
        )
        return (added.reshape(row_count, INNER), through_in[:, None, None] * incoming)

    (carried_out, _), pull_carried = jax.vjp(carried, reads_c, log_decay)
    output = (local_out + carried_out).astype(jnp.bfloat16)
    grad_x, grad_b, grad_c, grad_dt, grad_decay, grad_gain = pull_chain((upstream, adjoint_end))
    grad_c_extra, grad_decay_extra = pull_carried((upstream, adjoint_end))
    grad_tail, grad_rows, grad_weight, grad_bias, grad_dtb, grad_alog = pull_prep(
        (grad_x, grad_b, grad_c + grad_c_extra, grad_dt, grad_decay + grad_decay_extra)
    )
    returned = from_behind(grad_tail, "seq", -1)
    grad_rows = jnp.concatenate(
        [
            grad_rows[: row_count - CONV + 1],
            grad_rows[row_count - CONV + 1 :] + returned * keep_rows[:, None],
        ],
        axis=0,
    )
    summed = lax.psum((grad_weight, grad_bias, grad_dtb, grad_alog, grad_gain), ("dp", "seq"))
    scale = float(lax.axis_size("dp") * lax.axis_size("seq") * row_count) ** (-0.5)
    return (
        output,
        grad_rows.astype(jnp.bfloat16),
        summed[0] * scale,
        summed[1] * scale,
        summed[2] * scale,
        summed[3] * scale,
        summed[4] * scale,
    )


def solution(mesh):
    return jax.shard_map(
        on_device,
        mesh=mesh,
        in_specs=(
            P(("dp", "seq"), None),
            P(("dp", "seq")),
            P(),
            P(),
            P(("dp", "seq"), None),
            P(),
            P(),
            P(),
            P(("dp", "seq"), None),
        ),
        out_specs=(P(("dp", "seq"), None), P(("dp", "seq"), None), P(), P(), P(), P(), P()),
        check_vma=False,
    )
```

profile of v0, /device:TPU:1, one launch (start us, length us, event | category | flops | bytes accessed | tf_op | source)
XLA Modules:
  0.0 1133.3 jit_solution(11397604116379961711)
XLA Ops:
  9.4 4.6 collective-permute-start
  21.4 7.5 fusion.100
  31.3 5.1 reshape.509
  36.5 69.3 %while.76 = (s32[]{:T(128)}, f32[80,64,128]{2,1,0:T(8,128)S(1)}, f32[2,64,80,64]{3,2,1,0:T(8,128)}, f32[2,80,64,128]{3,2,1,0:T(8,128)}, f32[2,80]{1,0:T(2,128)S(...) while((s32[]{:T(128)}, f32[80,64,128]{2,1,0:T(8,128)S(1)}, ...), condition=%wide.region_5.6_spmd.clone, body=%wide.region_2.5_spmd.clone.sunk | while | flops 1271495936 | bytes 43904780 | solution.py:109
  38.4 3.7 fusion.191
  43.8 3.2 copy.213
  50.0 5.3 multiply_add_fusion.7
  55.8 8.7 fusion.194
  64.5 3.3 copy.219
  67.8 3.4 constant_dynamic-update-slice_fusion.4
  73.0 3.7 fusion.191
  78.3 3.2 copy.213
  84.6 5.3 multiply_add_fusion.7
  90.4 8.7 fusion.194
  99.1 3.3 copy.219
  102.3 3.4 constant_dynamic-update-slice_fusion.4
  114.3 21.7 %all-gather.2 = f32[32,1,80]{2,1,0:T(1,128)S(1)} all-gather(f32[1,1,80]{2,1,0:T(1,128)S(1)} %multiply_bitcast_fusion), channel_id=1, replica_groups=mesh['dp'=4,'seq'=32] {'seq'}, dimensions={0}, use_global_device_ids=true | all-gather | bytes 10560 | tf_op jit(solution)/shard_map/all_gather | solution.py:23
  136.0 218.2 %all-gather.6.cloned.1.call-done = f32[2560,64,128]{2,1,0:T(8,128)} async-done(((f32[80,64,128]{2,1,0:T(8,128)}), f32[2560,64,128]{2,1,0:T(8,128)}) %all-gather.6.cloned.1.call-update) | async-done | bytes 83886096 | tf_op jit(solution)/shard_map/all_gather | solution.py:23
  354.3 77.1 %while.77 = (s32[]{:T(128)}, f32[80,64,128]{2,1,0:T(8,128)S(1)}, s32[]{:T(128)}, f32[32,80]{1,0:T(8,128)S(1)}, f32[32,80,64,128]{3,2,1,0:T(8,128)}, /*index=5*/s32[]{:T(128)}, s32[]{:T(128)}) while((s32[]{:T(128)}, f32[80,64,128]{2,1,0:T(8,128)S(1)}, s32[]{:T(128)}, f32[32,80]{1,0:T(8,128)S(1)}, f32[32,80,64,128]{3,2,1,0:T(8,128)}, ...), condition=%wide.region_8.9_spmd.clone, body=%wide.region_7.8_spmd.clone.sunk | while | flops 2621444 | bytes 7865393 | solution.py:36
  431.3 8.7 multiply_reduce_fusion.10
  441.5 5.1 fusion.101
  446.7 6.0 reshape.542
  452.7 8.1 copy.125
  460.8 6.5 copy.124
  467.3 5.4 reshape.512
  472.7 4.2 copy.118
  477.0 3.3 copy.119
  481.0 3.9 add_convert_fusion
  484.9 205.6 %all-gather.8.cloned.1.call-done = f32[2560,64,128]{2,1,0:T(8,128)} async-done(((f32[80,64,128]{2,1,0:T(8,128)}), f32[2560,64,128]{2,1,0:T(8,128)}) %all-gather.8.cloned.1.call-update) | async-done | bytes 83886096 | tf_op jit(solution)/shard_map/all_gather | solution.py:23
  690.5 77.1 %while.78 = (s32[]{:T(128)}, f32[80,64,128]{2,1,0:T(8,128)S(1)}, s32[]{:T(128)}, f32[32,80]{1,0:T(8,128)S(1)}, f32[32,80,64,128]{3,2,1,0:T(8,128)}, /*index=5*/s32[]{:T(128)}, s32[]{:T(128)}, s32[]{:T(128)}, s32[]{:T(128)}) while((s32[]{:T(128)}, f32[80,64,128]{2,1,0:T(8,128)S(1)}, s32[]{:T(128)}, f32[32,80]{1,0:T(8,128)S(1)}, ...), condition=%wide.region_10.11_spmd.clone, body=%wide.region_9.10_spmd.clone.sunk | while | flops 2621448 | bytes 7865455 | solution.py:36
  772.6 176.0 %while.79 = (s32[]{:T(128)}, f32[80,64,128]{2,1,0:T(8,128)}, f32[80]{0:T(128)S(1)}, f32[2,64,80,64]{2,1,3,0:T(8,128)}, f32[2,64,128]{2,1,0:T(8,128)S(1)}, /*inde...) while((s32[]{:T(128)}, f32[80,64,128]{2,1,0:T(8,128)}, ...), condition=%wide.region_24.25_spmd.clone, body=%wide.region_11.24_spmd.clone.sunk | while | flops 3052656640 | bytes 114250048 | solution.py:109
  773.0 3.7 dynamic-slice_bitcast_fusion.21
  776.8 3.2 dynamic-slice_bitcast_fusion.22
  780.9 3.4 copy.226
  784.3 4.6 copy.230
  788.9 8.2 fusion.220
  797.3 9.1 multiply_reduce_fusion.17
  811.5 9.6 multiply_reduce_fusion.16
  821.3 4.1 fusion.223
  825.3 4.5 copy.225
  830.5 6.4 multiply_add_fusion.8
  836.9 6.5 fusion.219
  843.4 4.1 copy.229
  847.5 4.5 bitcast_dynamic-update-slice_fusion.7
  852.3 3.9 fusion.225
  857.1 3.7 dynamic-slice_bitcast_fusion.21
  864.9 3.4 copy.226
  868.3 4.7 copy.230
  873.0 8.2 fusion.220
  881.4 9.1 multiply_reduce_fusion.17
  895.6 9.6 multiply_reduce_fusion.16
  905.4 4.1 fusion.223
  909.5 4.7 copy.225
  914.8 6.4 multiply_add_fusion.8
  921.2 6.5 fusion.219
  927.7 3.8 copy.229
  931.6 4.5 bitcast_dynamic-update-slice_fusion.7
  936.3 3.9 fusion.225
  948.6 6.1 copy.127
  954.8 5.5 reshape.518
  960.3 7.3 fusion.110
  967.7 5.5 multiply_reduce_fusion.9
  986.6 66.0 %all-reduce.15 = (f32[5376]{0:T(1024)S(1)}, f32[80]{0:T(128)S(1)}, f32[80]{0:T(128)S(1)}, f32[80]{0:T(128)S(1)}) all-reduce(f32[5376]{0:T(1024)S(1)} %get-tuple-element.978, f32[80]{0:T(128)S(1)} %get-tuple-element.981, f32[80]{0:T(128)S(1)} %negate_multiply_fusion, ...), channel_id=1, replica_groups=mesh['dp'=4,'seq'=32] {'dp','seq'}, use_global_device_ids=true, to_apply=%region_31.32 | all-reduce | flops 5616 | bytes 44928 | tf_op jit(solution)/shard_map/psum | solution.py:201
  1057.0 65.2 %all-reduce.18.cloned.1.call-done = f32[4,5376]{1,0:T(4,128)} async-done(((f32[4,5376]{1,0:T(4,128)}), f32[4,5376]{1,0:T(4,128)}) %all-reduce.18.cloned.1.call-update) | async-done | bytes 86032 | tf_op jit(solution)/shard_map/psum | solution.py:201
  (425 shorter events, 233.5 us)
Async XLA Ops:
  7.2 14.3 %copy-start.37 = (f32[5376]{0:T(1024)S(1)}, f32[5376]{0:T(1024)}, u32[]{:S(2)}) copy-start(f32[5376]{0:T(1024)} %param.20) | copy-start | bytes 64516
  7.2 347.1 %all-gather.6.cloned.1.call-start = ((), (), s32[]{:S(2)}) async-start(), calls=%async_computation.1 | async-start | bytes 86507520 | tf_op jit(solution)/shard_map/all_gather | solution.py:23
  8.4 7.2 copy-start.50
  9.4 12.0 %collective-permute-start = (bf16[3,5376]{1,0:T(4,128)(2,1)S(1)}, bf16[3,5376]{1,0:T(4,128)(2,1)S(1)}, u32[]{:S(2)}, u32[]{:S(2)}) collective-permute-start(bf16[3,5376]{1,0:T(4,128)(2,1)S(1)} %slice_multiply_fusion), channel_id=1, source_target_pairs={{0,1},{1,2},{2,3},{3,4},{4,5},{5,6},{6,7},{7,8},{8,9},{9,10},{10,1... | collective-permute-start | bytes 96776 | tf_op jit(solution)/shard_map/ppermute | solution.py:18
  14.9 14.0 %copy-start.26 = (f32[128,80]{1,0:T(8,128)}, f32[128,80]{1,0:T(8,128)S(1)}, u32[]{:S(2)}) copy-start(f32[128,80]{1,0:T(8,128)S(1)} %copy.111) | copy-start | bytes 122884
  16.1 12.8 %copy-start.39 = (f32[128]{0:T(128)}, f32[128]{0:T(128)S(1)}, u32[]{:S(2)}) copy-start(f32[128]{0:T(128)S(1)} %get-tuple-element.1103) | copy-start | bytes 1540
  16.1 12.8 %copy-start.41 = (f32[128]{0:T(128)}, f32[128]{0:T(128)S(1)}, u32[]{:S(2)}) copy-start(f32[128]{0:T(128)S(1)} %get-tuple-element.1104) | copy-start | bytes 1540
  16.1 12.9 %copy-start.43 = (f32[128]{0:T(128)}, f32[128]{0:T(128)S(1)}, u32[]{:S(2)}) copy-start(f32[128]{0:T(128)S(1)} %get-tuple-element.1105) | copy-start | bytes 1540
  16.1 97.4 %copy-start.45 = (f32[128]{0:T(128)}, f32[128]{0:T(128)S(1)}, u32[]{:S(2)}) copy-start(f32[128]{0:T(128)S(1)} %get-tuple-element.1102) | copy-start | bytes 1540
  18.1 10.8 copy-start.29
  18.1 10.8 copy-start.31
  18.2 10.8 copy-start.33
  18.2 10.8 copy-start.35
  21.4 7.6 copy-start.22
  29.0 2.3 copy-start.19
  31.3 5.2 copy-start.38
  38.4 3.7 copy-start.9
  73.0 3.7 copy-start.9
  105.8 1.5 copy-start.3
  107.3 583.2 %all-gather.8.cloned.1.call-start = ((), (), s32[]{:S(2)}) async-start(), calls=%async_computation.2 | async-start | bytes 86507520 | tf_op jit(solution)/shard_map/all_gather | solution.py:23
  112.9 241.4 %copy-start.24 = (f32[128,80]{1,0:T(8,128)}, f32[128,80]{1,0:T(8,128)S(1)}, u32[]{:S(2)}) copy-start(f32[128,80]{1,0:T(8,128)S(1)} %reduce_window_sum.84) | copy-start | bytes 122884
  431.3 8.7 copy-start.5
  440.0 1.5 copy-start.18
  446.6 675.6 %all-reduce.18.cloned.1.call-start = ((), (), s32[]{:S(2)}) async-start(), calls=%async_computation | async-start | bytes 172032 | tf_op jit(solution)/shard_map/psum | solution.py:201
  767.6 2.4 copy-start.7
  773.0 3.7 copy-start.11
  797.3 9.1 copy-start
  806.4 5.2 copy-start.2
  830.5 6.4 copy-start.10
  847.5 4.8 copy-start.1
  847.5 4.8 copy-start.4
  857.1 3.7 copy-start.11
  881.3 9.1 copy-start
  890.4 5.2 copy-start.2
  914.8 6.4 copy-start.10
  931.5 4.8 copy-start.1
  931.6 4.8 copy-start.4
  954.8 5.5 copy-start.6
  954.8 12.9 %copy-start.23 = (f32[3,5376]{1,0:T(4,128)S(1)}, f32[3,5376]{1,0:T(4,128)}, u32[]{:S(2)}) copy-start(f32[3,5376]{1,0:T(4,128)} %copy-done.22) | copy-start | bytes 193540
  960.3 7.4 copy-start.17
  960.3 7.4 copy-start.20
  960.3 7.4 copy-start.40
  960.3 7.4 copy-start.42
  960.3 7.4 copy-start.44
  967.7 5.6 copy-start.30
  967.7 5.6 copy-start.32
  967.7 5.6 copy-start.34
  967.7 5.6 copy-start.36
  974.3 1.6 copy-start.12
  974.3 2.4 copy-start.14
  974.3 3.2 copy-start.15
  974.3 4.0 copy-start.16
  978.3 2.0 copy-start.8
  980.3 4.3 copy-start.25
  980.3 5.0 copy-start.28
  980.3 5.0 copy-start.46
  980.3 6.2 copy-start.27
  980.3 6.2 copy-start.47
  980.3 6.2 copy-start.49
  980.3 6.3 copy-start.52
  981.0 142.8 %copy-start.13 = (f32[128,5376]{1,0:T(8,128)S(1)}, f32[128,5376]{1,0:T(8,128)}, u32[]{:S(2)}) copy-start(f32[128,5376]{1,0:T(8,128)} %copy-done.12) | copy-start | bytes 8257540
  981.0 142.8 %copy-start.51 = (f32[3]{0:T(128)S(1)}, f32[3]{0:T(128)}, u32[]{:S(2)}) copy-start(f32[3]{0:T(128)} %copy-done.50) | copy-start | bytes 40
  981.0 142.8 %collective-permute-start.1 = (f32[3,5376]{1,0:T(4,128)S(1)}, f32[3,5376]{1,0:T(4,128)S(1)}, u32[]{:S(2)}, u32[]{:S(2)}) collective-permute-start(f32[3,5376]{1,0:T(4,128)S(1)} %pad_add_fusion.1), channel_id=1, source_target_pairs={{1,0},{2,1},{3,2},{4,3},{5,4},{6,5},{7,6},{8,7},{9,8},{10,9},{11,1... | collective-permute-start | bytes 193544 | tf_op jit(solution)/shard_map/ppermute | solution.py:18
  1123.7 1.6 copy-start.21
  (1 other events, 0.5 us)
Sparse Core Ops, SparseCore 0:
  107.4 246.8 all-gather.5
  446.8 243.7 all-gather.7
  984.7 137.4 all-reduce.17
where the time goes:
time: 1140 us; the launch traced here: 1130 us
  waiting for transfers between devices  489 us (43%)
  other arithmetic  218 us (19%)
  matrix products  153 us (13%)
  local copies, waits for them, and re-layouts  151 us (13%)
  blocking collectives  87.7 us (8%)
  between operations  14.8 us (1%)
  loops' own time  12 us (1%)
    all_gather x2, waiting for transfers between devices, prefix(): everything = jax.tree.map(lambda part: lax.all_gather(part, axis), array)  424 us
    select_n x64, other arithmetic, step(): return jax.tree.map(lambda a, b: jnp.where(reached, a, b), new, before)  151 us
    psum x1, blocking collectives, on_device(): lax.psum((grad_weight, grad_bias, grad_dtb, grad_alog, grad_gain), ('dp',...  66 us
    psum x1, waiting for transfers between devices, on_device(): lax.psum((grad_weight, grad_bias, grad_dtb, grad_alog, grad_gain), ('dp',...  65.2 us
    dot_general x6, matrix products, scan_block(): output = jnp.einsum('hts,shp->thp', weights, values_x, precision=exact_mode)  46.7 us
    dot_general x8, matrix products, scan_block(): jnp.einsum('tn,hpn->thp', reads_c, carry_state, precision=exact_mode)  46.1 us
    dot_general x6, matrix products, scan_block(): jnp.einsum('shp,sn->hpn', leave_weight[:, :, None] * values_x, keys_b, pr...  37.8 us
    unnamed x97, local copies, waits for them, and re-layouts  28 us
  transfers between devices with their start and end apart: 5, of which 3 were waited for; matrix products, arithmetic and copies ran while one was open for 5% of the time, Pallas kernels for 0%

commit v1 on v0

--- a/solution.py
+++ b/solution.py
@@ -198,7 +198,8 @@
         ],
         axis=0,
     )
-    summed = lax.psum((grad_weight, grad_bias, grad_dtb, grad_alog, grad_gain), ("dp", "seq"))
+    partial = lax.psum((grad_weight, grad_bias, grad_dtb, grad_alog, grad_gain), "dp")
+    summed = lax.psum(partial, "seq")
     scale = float(lax.axis_size("dp") * lax.axis_size("seq") * row_count) ** (-0.5)
     return (
         output,

time: 1140 us -> 1280 us (1.12)
  waiting for transfers between devices: 489 us -> 562 us
  blocking collectives: 87.7 us -> 156 us
    psum x1 -> x2, waiting for transfers between devices: 65.2 us -> 138 us  [the longest x1 101 us: on_device(): summed = lax.psum(partial, 'seq')]
    psum x1 -> x2, blocking collectives: 66 us -> 135 us  [the longest x1 121 us: on_device(): summed = lax.psum(partial, 'seq')]
    unnamed x97 -> x95, local copies, waits for them, and re-layouts: 28 us -> 27.7 us
  transfers between devices with their start and end apart: 5 -> 6, of which waited for: 3 -> 4; matrix products, arithmetic and copies ran while one was open for 5% -> 5% of each run, Pallas kernels for 0% -> 0%
where the time goes in v1:
time: 1280 us
  waiting for transfers between devices  562 us (44%)
  other arithmetic  219 us (17%)
  blocking collectives  156 us (12%)
  matrix products  153 us (12%)
  local copies, waits for them, and re-layouts  151 us (12%)
  between operations  14.8 us (1%)
    all_gather x2, waiting for transfers between devices, prefix(): everything = jax.tree.map(lambda part: lax.all_gather(part, axis), array)  424 us
    select_n x64, other arithmetic, step(): return jax.tree.map(lambda a, b: jnp.where(reached, a, b), new, before)  151 us
    psum x1, blocking collectives, on_device(): summed = lax.psum(partial, 'seq')  121 us
    psum x1, waiting for transfers between devices, on_device(): summed = lax.psum(partial, 'seq')  101 us
    dot_general x6, matrix products, scan_block(): output = jnp.einsum('hts,shp->thp', weights, values_x, precision=exact_mode)  46.7 us
    dot_general x8, matrix products, scan_block(): jnp.einsum('tn,hpn->thp', reads_c, carry_state, precision=exact_mode)  46.1 us
    dot_general x6, matrix products, scan_block(): jnp.einsum('shp,sn->hpn', leave_weight[:, :, None] * values_x, keys_b, pr...  37.8 us
    psum x1, waiting for transfers between devices, on_device(): lax.psum((grad_weight, grad_bias, grad_dtb, grad_alog, grad_gain), 'dp')  36.8 us
  transfers between devices with their start and end apart: 6, of which 4 were waited for; matrix products, arithmetic and copies ran while one was open for 5% of the time, Pallas kernels for 0%

profile of v1, /device:TPU:1, one launch (start us, length us, event | category | flops | bytes accessed | tf_op | source)
XLA Modules:
  0.0 1275.4 jit_solution(3335038050490632153)
XLA Ops:
  9.4 4.6 collective-permute-start
  21.4 7.5 fusion.100
  31.3 5.1 reshape.509
  36.5 69.3 %while.76 = (s32[]{:T(128)}, f32[80,64,128]{2,1,0:T(8,128)S(1)}, f32[2,64,80,64]{3,2,1,0:T(8,128)}, f32[2,80,64,128]{3,2,1,0:T(8,128)}, f32[2,80]{1,0:T(2,128)S(...) while((s32[]{:T(128)}, f32[80,64,128]{2,1,0:T(8,128)S(1)}, ...), condition=%wide.region_5.6_spmd.clone, body=%wide.region_2.5_spmd.clone.sunk | while | flops 1271495936 | bytes 43904780 | solution.py:109
  38.4 3.7 fusion.191
  50.0 5.3 multiply_add_fusion.7
  55.8 8.7 fusion.194
  64.5 3.3 copy.219
  67.8 3.4 constant_dynamic-update-slice_fusion.4
  73.0 3.7 fusion.191
  78.3 3.2 copy.213
  84.6 5.3 multiply_add_fusion.7
  90.4 8.7 fusion.194
  99.1 3.3 copy.219
  102.3 3.4 constant_dynamic-update-slice_fusion.4
  114.3 21.7 %all-gather.2 = f32[32,1,80]{2,1,0:T(1,128)S(1)} all-gather(f32[1,1,80]{2,1,0:T(1,128)S(1)} %multiply_bitcast_fusion), channel_id=1, replica_groups=mesh['dp'=4,'seq'=32] {'seq'}, dimensions={0}, use_global_device_ids=true | all-gather | bytes 10560 | tf_op jit(solution)/shard_map/all_gather | solution.py:23
  136.0 218.2 %all-gather.6.cloned.1.call-done = f32[2560,64,128]{2,1,0:T(8,128)} async-done(((f32[80,64,128]{2,1,0:T(8,128)}), f32[2560,64,128]{2,1,0:T(8,128)}) %all-gather.6.cloned.1.call-update) | async-done | bytes 83886096 | tf_op jit(solution)/shard_map/all_gather | solution.py:23
  354.3 77.1 %while.77 = (s32[]{:T(128)}, f32[80,64,128]{2,1,0:T(8,128)S(1)}, s32[]{:T(128)}, f32[32,80]{1,0:T(8,128)S(1)}, f32[32,80,64,128]{3,2,1,0:T(8,128)}, /*index=5*/s32[]{:T(128)}, s32[]{:T(128)}) while((s32[]{:T(128)}, f32[80,64,128]{2,1,0:T(8,128)S(1)}, s32[]{:T(128)}, f32[32,80]{1,0:T(8,128)S(1)}, f32[32,80,64,128]{3,2,1,0:T(8,128)}, ...), condition=%wide.region_8.9_spmd.clone, body=%wide.region_7.8_spmd.clone.sunk | while | flops 2621444 | bytes 7865393 | solution.py:36
  431.3 8.7 multiply_reduce_fusion.10
  441.5 5.1 fusion.101
  446.7 6.0 reshape.542
  452.7 8.1 copy.125
  460.8 6.5 copy.124
  467.3 5.4 reshape.512
  472.7 4.2 copy.118
  477.0 3.3 copy.119
  481.0 3.9 add_convert_fusion
  484.9 205.6 %all-gather.8.cloned.1.call-done = f32[2560,64,128]{2,1,0:T(8,128)} async-done(((f32[80,64,128]{2,1,0:T(8,128)}), f32[2560,64,128]{2,1,0:T(8,128)}) %all-gather.8.cloned.1.call-update) | async-done | bytes 83886096 | tf_op jit(solution)/shard_map/all_gather | solution.py:23
  690.5 77.1 %while.78 = (s32[]{:T(128)}, f32[80,64,128]{2,1,0:T(8,128)S(1)}, s32[]{:T(128)}, f32[32,80]{1,0:T(8,128)S(1)}, f32[32,80,64,128]{3,2,1,0:T(8,128)}, /*index=5*/s32[]{:T(128)}, s32[]{:T(128)}, s32[]{:T(128)}, s32[]{:T(128)}) while((s32[]{:T(128)}, f32[80,64,128]{2,1,0:T(8,128)S(1)}, s32[]{:T(128)}, f32[32,80]{1,0:T(8,128)S(1)}, ...), condition=%wide.region_10.11_spmd.clone, body=%wide.region_9.10_spmd.clone.sunk | while | flops 2621448 | bytes 7865455 | solution.py:36
  772.6 176.0 %while.79 = (s32[]{:T(128)}, f32[80,64,128]{2,1,0:T(8,128)}, f32[80]{0:T(128)S(1)}, f32[2,64,80,64]{2,1,3,0:T(8,128)}, f32[2,64,128]{2,1,0:T(8,128)S(1)}, /*inde...) while((s32[]{:T(128)}, f32[80,64,128]{2,1,0:T(8,128)}, ...), condition=%wide.region_24.25_spmd.clone, body=%wide.region_11.24_spmd.clone.sunk | while | flops 3052656640 | bytes 114250048 | solution.py:109
  773.0 3.7 dynamic-slice_bitcast_fusion.21
  780.9 3.4 copy.226
  784.3 4.6 copy.230
  788.9 8.2 fusion.220
  797.3 9.1 multiply_reduce_fusion.17
  811.5 9.6 multiply_reduce_fusion.16
  821.3 4.1 fusion.223
  825.3 4.5 copy.225
  830.5 6.4 multiply_add_fusion.8
  836.9 6.5 fusion.219
  843.4 4.1 copy.229
  847.5 4.5 bitcast_dynamic-update-slice_fusion.7
  852.3 3.9 fusion.225
  857.1 3.7 dynamic-slice_bitcast_fusion.21
  864.9 3.4 copy.226
  868.3 4.7 copy.230
  873.0 8.2 fusion.220
  881.4 9.1 multiply_reduce_fusion.17
  895.6 9.6 multiply_reduce_fusion.16
  905.4 4.1 fusion.223
  909.5 4.7 copy.225
  914.8 6.4 multiply_add_fusion.8
  921.2 6.5 fusion.219
  927.7 3.8 copy.229
  931.6 4.5 bitcast_dynamic-update-slice_fusion.7
  936.3 3.9 fusion.225
  948.6 6.1 copy.127
  954.8 5.5 reshape.518
  960.3 7.3 fusion.110
  967.7 5.5 multiply_reduce_fusion.9
  985.9 13.4 %all-reduce.16 = (f32[5376]{0:T(1024)S(1)}, f32[80]{0:T(128)S(1)}, f32[80]{0:T(128)S(1)}, f32[80]{0:T(128)S(1)}) all-reduce(f32[5376]{0:T(1024)S(1)} %get-tuple-element.978, f32[80]{0:T(128)S(1)} %get-tuple-element.981, f32[80]{0:T(128)S(1)} %negate_multiply_fusion, ...), channel_id=1, replica_groups=mesh['dp'=4,'seq'=32] {'dp'}, use_global_device_ids=true, to_apply=%region_32.33 | all-reduce | flops 5616 | bytes 44928 | tf_op jit(solution)/shard_map/psum | solution.py:201
  999.3 121.1 %all-reduce.15 = (f32[5376]{0:T(1024)S(1)}, f32[80]{0:T(128)S(1)}, f32[80]{0:T(128)S(1)}, f32[80]{0:T(128)S(1)}) all-reduce(f32[5376]{0:T(1024)S(1)} %get-tuple-element.1068, f32[80]{0:T(128)S(1)} %get-tuple-element.1069, f32[80]{0:T(128)S(1)} %get-tuple-element.1070, ...), channel_id=1, replica_groups=mesh['dp'=4,'seq'=32] {'seq'}, use_global_device_ids=true, to_apply=%region_33.34 | all-reduce | flops 5616 | bytes 44928 | tf_op jit(solution)/shard_map/psum | solution.py:202
  1126.8 36.8 %all-reduce.20.cloned.1.call-done = f32[4,5376]{1,0:T(4,128)} async-done(((f32[4,5376]{1,0:T(4,128)}), f32[4,5376]{1,0:T(4,128)}) %all-reduce.20.cloned.1.call-update) | async-done | bytes 86032 | tf_op jit(solution)/shard_map/psum | solution.py:201
  1166.1 100.9 %all-reduce.22.cloned.1.call-done = f32[4,5376]{1,0:T(4,128)} async-done(((f32[4,5376]{1,0:T(4,128)}), f32[4,5376]{1,0:T(4,128)}) %all-reduce.22.cloned.1.call-update) | async-done | bytes 86032 | tf_op jit(solution)/shard_map/psum | solution.py:202
  (427 shorter events, 241.0 us)
Async XLA Ops:
  7.2 14.3 %copy-start.36 = (f32[5376]{0:T(1024)S(1)}, f32[5376]{0:T(1024)}, u32[]{:S(2)}) copy-start(f32[5376]{0:T(1024)} %param.20) | copy-start | bytes 64516
  7.2 347.1 %all-gather.6.cloned.1.call-start = ((), (), s32[]{:S(2)}) async-start(), calls=%async_computation.2 | async-start | bytes 86507520 | tf_op jit(solution)/shard_map/all_gather | solution.py:23
  8.4 7.2 copy-start.49
  9.4 12.0 collective-permute-start
  14.9 14.0 %copy-start.25 = (f32[128,80]{1,0:T(8,128)}, f32[128,80]{1,0:T(8,128)S(1)}, u32[]{:S(2)}) copy-start(f32[128,80]{1,0:T(8,128)S(1)} %copy.111) | copy-start | bytes 122884
  16.1 12.8 %copy-start.38 = (f32[128]{0:T(128)}, f32[128]{0:T(128)S(1)}, u32[]{:S(2)}) copy-start(f32[128]{0:T(128)S(1)} %get-tuple-element.1107) | copy-start | bytes 1540
  16.1 12.8 %copy-start.40 = (f32[128]{0:T(128)}, f32[128]{0:T(128)S(1)}, u32[]{:S(2)}) copy-start(f32[128]{0:T(128)S(1)} %get-tuple-element.1108) | copy-start | bytes 1540
  16.1 12.9 %copy-start.42 = (f32[128]{0:T(128)}, f32[128]{0:T(128)S(1)}, u32[]{:S(2)}) copy-start(f32[128]{0:T(128)S(1)} %get-tuple-element.1109) | copy-start | bytes 1540
  16.1 97.4 %copy-start.44 = (f32[128]{0:T(128)}, f32[128]{0:T(128)S(1)}, u32[]{:S(2)}) copy-start(f32[128]{0:T(128)S(1)} %get-tuple-element.1106) | copy-start | bytes 1540
  18.1 10.8 copy-start.28
  18.1 10.8 copy-start.30
  18.2 10.8 copy-start.32
  18.2 10.8 copy-start.34
  21.4 7.6 copy-start.21
  29.0 2.3 copy-start.19
  31.3 5.2 copy-start.37
  38.4 3.7 copy-start.9
  73.0 3.7 copy-start.9
  105.8 1.5 copy-start.3
  107.3 583.2 %all-gather.8.cloned.1.call-start = ((), (), s32[]{:S(2)}) async-start(), calls=%async_computation.3 | async-start | bytes 86507520 | tf_op jit(solution)/shard_map/all_gather | solution.py:23
  112.9 241.4 %copy-start.23 = (f32[128,80]{1,0:T(8,128)}, f32[128,80]{1,0:T(8,128)S(1)}, u32[]{:S(2)}) copy-start(f32[128,80]{1,0:T(8,128)S(1)} %reduce_window_sum.84) | copy-start | bytes 122884
  431.3 8.7 copy-start.5
  440.0 1.5 copy-start.18
  446.6 716.9 %all-reduce.20.cloned.1.call-start = ((), (), s32[]{:S(2)}) async-start(), calls=%async_computation | async-start | bytes 172032 | tf_op jit(solution)/shard_map/psum | solution.py:201
  767.6 2.4 copy-start.7
  773.0 3.7 copy-start.11
  797.3 9.1 copy-start
  806.4 5.2 copy-start.2
  830.5 6.4 copy-start.10
  847.5 4.8 copy-start.1
  847.5 4.8 copy-start.4
  857.1 3.7 copy-start.11
  881.3 9.1 copy-start
  890.4 5.2 copy-start.2
  914.8 6.4 copy-start.10
  931.5 4.8 copy-start.1
  931.6 4.8 copy-start.4
  954.8 5.5 copy-start.6
  954.8 12.9 %copy-start.22 = (f32[3,5376]{1,0:T(4,128)S(1)}, f32[3,5376]{1,0:T(4,128)}, u32[]{:S(2)}) copy-start(f32[3,5376]{1,0:T(4,128)} %copy-done.21) | copy-start | bytes 193540
  960.3 7.4 copy-start.17
  960.3 7.4 copy-start.20
  960.3 7.4 copy-start.39
  960.3 7.4 copy-start.41
  960.3 7.4 copy-start.43
  967.7 5.6 copy-start.29
  967.7 5.6 copy-start.31
  967.7 5.6 copy-start.33
  967.7 5.6 copy-start.35
  974.3 1.6 copy-start.12
  974.3 2.4 copy-start.14
  974.3 3.2 copy-start.15
  974.3 4.0 copy-start.16
  978.2 2.0 copy-start.8
  980.3 3.6 copy-start.24
  980.3 4.2 copy-start.27
  980.3 4.2 copy-start.45
  980.3 5.4 copy-start.26
  980.3 5.4 copy-start.46
  980.3 5.4 copy-start.48
  980.3 5.5 copy-start.51
  981.0 144.6 %copy-start.13 = (f32[128,5376]{1,0:T(8,128)S(1)}, f32[128,5376]{1,0:T(8,128)}, u32[]{:S(2)}) copy-start(f32[128,5376]{1,0:T(8,128)} %copy-done.12) | copy-start | bytes 8257540
  981.0 144.6 %copy-start.50 = (f32[3]{0:T(128)S(1)}, f32[3]{0:T(128)}, u32[]{:S(2)}) copy-start(f32[3]{0:T(128)} %copy-done.49) | copy-start | bytes 40
  981.0 144.6 %collective-permute-start.1 = (f32[3,5376]{1,0:T(4,128)S(1)}, f32[3,5376]{1,0:T(4,128)S(1)}, u32[]{:S(2)}, u32[]{:S(2)}) collective-permute-start(f32[3,5376]{1,0:T(4,128)S(1)} %pad_add_fusion.1), channel_id=1, source_target_pairs={{1,0},{2,1},{3,2},{4,3},{5,4},{6,5},{7,6},{8,7},{9,8},{10,9},{11,1... | collective-permute-start | bytes 193544 | tf_op jit(solution)/shard_map/ppermute | solution.py:18
  1125.5 141.5 %all-reduce.22.cloned.1.call-start = ((), (), s32[]{:S(2)}) async-start(), calls=%async_computation.1 | async-start | bytes 172032 | tf_op jit(solution)/shard_map/psum | solution.py:202
  (1 other events, 0.5 us)
Sparse Core Ops, SparseCore 0:
  107.4 246.8 all-gather.5
  446.8 243.7 all-gather.7
  1125.7 37.8 all-reduce.19
  1167.0 99.9 all-reduce.21
